TPU v7x, 32 devices: a whole 2x2x4 slice. The times are simulated.
32 devices in a mesh: blk: 8 (over z, y), rep: 4 (over x, core).
Axes of the slice: x: 2, y: 2, z: 4, core: 2. Of those that a mesh axis runs over, the one named last changes fastest.
Arguments:
- resident_keys: int32 [16384], P('blk'), may hold values from 0 to 4095
- moving_keys: int32 [65536], P(('blk', 'rep')), may hold values from 0 to 4095
- payload: float32 [65536, 128], P(('blk', 'rep')), may hold values from -6 to 6
Outputs:
- joined: float32 [16384, 128], P(('blk', 'rep'))
All inputs are finite; a program needn't handle non-finite values.
Results may differ from a plain program's by a relative error of at most 0.0003.
Values sent between devices are 32-bit elements; how exact they have to be, the bound alone decides.
A program may use at most 64 MiB of HBM per device.

v0:
```python
import functools

import jax
import jax.numpy as jnp
from jax import lax
from jax.experimental import pallas as pl
from jax.experimental.pallas import tpu as pltpu
from jax.sharding import PartitionSpec as P

REACH = 2
LANES = 128
CHUNK = 2048


def kernel(
    n_blk, groups, rk_ref, mk_ref, pay_ref, out_ref,
    pay, other_pay, mkeys, rkeys, hl, kcol, abuf, xrecv, bbuf, sbuf, brecv, yrecv,
    in_sem, key_send, key_recv, pair_send, pair_recv, x_send, x_recv, b_send, b_recv, y_send, y_recv,
):
    blk = lax.axis_index("blk")
    rep = lax.axis_index("rep")
    group, core = rep // 2, rep % 2
    rows, width = pay.shape
    quarter = out_ref.shape[0]
    key_rows = mk_ref.shape[0]
    qrows = quarter // LANES
    fold = n_blk % 2 == 0
    near = 2 * (blk % 2) - 1 if fold else -1
    offs = [REACH, -REACH, near, -near]
    key_to = [-REACH, REACH] + ([near, -near] if fold else [-near, near])
    own = len(offs)

    def at(off):
        return lax.rem(blk + off + n_blk, n_blk)

    mate = rep + 1 - 2 * core
    peers = [lax.rem(group + d, groups) * 2 + core for d in range(1, groups)]

    load_pay = pltpu.make_async_copy(pay_ref, pay, in_sem.at[0])
    load_mk = pltpu.make_async_copy(mk_ref, mkeys.at[pl.ds(0, key_rows)], in_sem.at[1])
    load_rk = pltpu.make_async_copy(rk_ref, rkeys.at[own], in_sem.at[2])
    for c in (load_pay, load_mk, load_rk):
        c.start()

    barrier = pltpu.get_barrier_semaphore()
    for o in offs:
        pl.semaphore_signal(barrier, inc=1, device_id={"blk": at(o)})
    for p in peers + [mate]:
        pl.semaphore_signal(barrier, inc=1, device_id={"rep": p})
    pl.semaphore_wait(barrier, 1 + len(peers) + own)

    sent = []

    def send(src, dst, send_sem, recv_sem, to):
        c = pltpu.make_async_remote_copy(
            src_ref=src, dst_ref=dst, send_sem=send_sem, recv_sem=recv_sem, device_id=to)
        c.start()
        sent.append(c)
        return c

    keys = {}
    for i in (0, 3, 2, 1):
        keys[i] = send(rk_ref, rkeys.at[i], key_send.at[i], key_recv.at[i], {"blk": at(key_to[i])})
    pair_keys = send(mk_ref, mkeys.at[pl.ds(key_rows, key_rows)], pair_send.at[0], pair_recv.at[0], {"rep": mate})
    pair_pay = send(pay_ref, other_pay, pair_send.at[1], pair_recv.at[1], {"rep": mate})

    def split(src, base):
        @pl.loop(0, rows // 256)
        def _(k):
            v = src[pl.ds(k * 256, 256), :]
            hi = v.astype(jnp.bfloat16)
            lo = (v - hi.astype(jnp.float32)).astype(jnp.bfloat16)
            hl[pl.ds(base + k * 256, 256), 0:width] = hi
            hl[pl.ds(base + k * 256, 256), width:2 * width] = lo

    for c in (load_pay, load_mk, load_rk):
        c.wait()
    split(pay, 0)
    pair_keys.wait_recv()
    pair_pay.wait_recv()
    split(other_pay, rows)

    per = CHUNK // LANES

    def partial(slot, q):
        for j in range(qrows):
            row = rkeys[slot, pl.ds(q * qrows + j, 1), :]
            kcol[j * LANES:(j + 1) * LANES, :] = jnp.broadcast_to(row, (LANES, LANES)).T

        def part(k):
            mine = kcol[...]
            hot = []
            for g in range(per):
                row = mkeys[pl.ds(k * per + g, 1), :]
                hot.append(jnp.where(mine == row, 1.0, 0.0).astype(jnp.bfloat16))
            both = jnp.dot(jnp.concatenate(hot, axis=1), hl[pl.ds(k * CHUNK, CHUNK), :],
                           preferred_element_type=jnp.float32)
            return both[:, 0:width] + both[:, width:2 * width]

        return part, 2 * rows // CHUNK

    def compute(slot, q, dst):
        part, steps = partial(slot, q)
        if steps == 1:
            dst[...] = part(0)
            return
        dst[...] = part(0)

        @pl.loop(1, steps)
        def _(k):
            dst[...] += part(k)

    waiting = {}

    def send_x(i):
        waiting[i] = [
            send(abuf.at[i, d], xrecv.at[i, d], x_send.at[i, d], x_recv.at[i, d], {"rep": p})
            for d, p in enumerate(peers)]

    ready = set()

    def for_peers(i):
        if i != own and i not in ready:
            keys[i].wait_recv()
            ready.add(i)
        for d, p in enumerate(peers):
            compute(i, p, abuf.at[i, d])

    def for_me(i):
        compute(i, rep, bbuf.at[i])

    def finish(i):
        total = bbuf[i]
        for d, c in enumerate(waiting[i]):
            c.wait_recv()
            total = total + xrecv[i, d]
        return total

    def give(i):
        sbuf[i] = finish(i)
        return send(sbuf.at[i], brecv.at[i], b_send.at[i], b_recv.at[i], {"blk": at(offs[i])})

    def give_partner(src, d):
        return send(src, yrecv.at[d], y_send.at[d], y_recv.at[d], {"blk": at(offs[3])})

    for_peers(0)
    send_x(0)
    for_peers(3)
    if fold:
        folded = [give_partner(abuf.at[3, d], d) for d in range(groups - 1)]
    else:
        send_x(3)
    for_me(0)
    for_peers(2)
    send_x(2)
    given = [give(0)]
    for_peers(1)
    send_x(1)
    for_me(3)
    if fold:
        last = give_partner(bbuf.at[3], groups - 1)
    for_me(2)
    for_peers(own)
    if fold:
        for d, c in enumerate(folded):
            c.wait_recv()
            abuf[own, d] = abuf[own, d] + yrecv[d]
    send_x(own)
    given.append(give(2))
    for_me(1)
    if not fold:
        given.append(give(3))
    for_me(own)
    given.append(give(1))
    total = bbuf[own]
    if fold:
        last.wait_recv()
        total = total + yrecv[groups - 1]
    bbuf[own] = total
    total = finish(own)
    for i, c in zip((0, 2, 1) if fold else (0, 2, 3, 1), given):
        c.wait_recv()
        total = total + brecv[i]
    out_ref[...] = total
    for c in sent:
        c.wait_send()


def solution(mesh):
    n_blk, n_rep = mesh.shape["blk"], mesh.shape["rep"]
    groups = n_rep // 2
    slots = 4

    def local(resident_keys, moving_keys, payload):
        res, rows, width = resident_keys.shape[0], payload.shape[0], payload.shape[1]
        quarter = res // n_rep
        f32, bf16, i32 = jnp.float32, jnp.bfloat16, jnp.int32
        vmem = pl.BlockSpec(memory_space=pltpu.VMEM)
        dma = pltpu.SemaphoreType.DMA
        return pl.pallas_call(
            functools.partial(kernel, n_blk, groups),
            out_shape=jax.ShapeDtypeStruct((quarter, width), f32),
            in_specs=[pl.BlockSpec(memory_space=pl.ANY)] * 3,
            out_specs=vmem,
            scratch_shapes=[
                pltpu.VMEM((rows, width), f32),
                pltpu.VMEM((rows, width), f32),
                pltpu.VMEM((2 * rows // LANES, LANES), i32),
                pltpu.VMEM((slots + 1, res // LANES, LANES), i32),
                pltpu.VMEM((2 * rows, 2 * width), bf16),
                pltpu.VMEM((quarter, LANES), i32),
                pltpu.VMEM((slots + 1, groups - 1, quarter, width), f32),
                pltpu.VMEM((slots + 1, groups - 1, quarter, width), f32),
                pltpu.VMEM((slots + 1, quarter, width), f32),
                pltpu.VMEM((slots, quarter, width), f32),
                pltpu.VMEM((slots, quarter, width), f32),
                pltpu.VMEM((groups, quarter, width), f32),
                dma((3,)),
                dma((slots,)), dma((slots,)),
                dma((2,)), dma((2,)),
                dma((slots + 1, groups - 1)), dma((slots + 1, groups - 1)),
                dma((slots,)), dma((slots,)),
                dma((groups,)), dma((groups,)),
            ],
            compiler_params=pltpu.CompilerParams(
                collective_id=0, has_side_effects=True, vmem_limit_bytes=48 * 1024 * 1024),
        )(resident_keys.reshape(res // LANES, LANES), moving_keys.reshape(rows // LANES, LANES), payload)

    in_specs = (P("blk"), P(("blk", "rep")), P(("blk", "rep"), None))
    out_specs = P(("blk", "rep"), None)
    return jax.shard_map(local, mesh=mesh, in_specs=in_specs, out_specs=out_specs, check_vma=False)
```

profile of v0, /device:TPU:0, one launch (start us, length us, event | category | flops | bytes accessed | tf_op | source)
XLA Modules:
  0.0 40.2 jit_solution(7525331939811307429)
XLA Ops:
  0.0 0.0 copy-start
  0.0 1.2 %copy-done = f32[2048,128]{1,0:T(8,128)S(1)} copy-done((f32[2048,128]{1,0:T(8,128)S(1)}, f32[2048,128]{1,0:T(8,128)}, u32[]{:S(2)}) %copy-start) | copy-done | bytes 1048600
  1.2 0.0 copy-start.1
  1.2 0.7 %copy-done.1 = s32[2048]{0:T(1024)S(1)} copy-done((s32[2048]{0:T(1024)S(1)}, s32[2048]{0:T(1024)}, u32[]{:S(2)}) %copy-start.1) | copy-done | bytes 8216
  1.9 0.0 copy-start.2
  1.9 0.7 %copy-done.2 = s32[2048]{0:T(1024)S(1)} copy-done((s32[2048]{0:T(1024)S(1)}, s32[2048]{0:T(1024)}, u32[]{:S(2)}) %copy-start.2) | copy-done | bytes 8216
  2.6 36.9 %shard_map.37 = f32[512,128]{1,0:T(8,128)S(1)} custom-call(s32[16,128]{1,0:T(8,128)S(1)} %bitcast.2, s32[16,128]{1,0:T(8,128)S(1)} %bitcast.3, f32[2048,128]{1,0:T(8,128)S(1)} %copy-done), custom_call_target="tpu_custom_call" | custom-call | tf_op jit(solution)/shard_map/pallas_call | solution.py:200
  39.5 0.7 %copy.5 = f32[512,128]{1,0:T(8,128)} copy(f32[512,128]{1,0:T(8,128)S(1)} %shard_map.37) | data formatting | bytes 524288
Async XLA Ops:
  0.0 1.2 %copy-start = (f32[2048,128]{1,0:T(8,128)S(1)}, f32[2048,128]{1,0:T(8,128)}, u32[]{:S(2)}) copy-start(f32[2048,128]{1,0:T(8,128)} %pay_ref.1) | copy-start | bytes 3145732
  1.2 0.7 %copy-start.1 = (s32[2048]{0:T(1024)S(1)}, s32[2048]{0:T(1024)}, u32[]{:S(2)}) copy-start(s32[2048]{0:T(1024)} %param.3) | copy-start | bytes 24580
  1.9 0.7 %copy-start.2 = (s32[2048]{0:T(1024)S(1)}, s32[2048]{0:T(1024)}, u32[]{:S(2)}) copy-start(s32[2048]{0:T(1024)} %param.4) | copy-start | bytes 24580
where the time goes:
time: 40.5 us; the launch traced here: 40.2 us
  Pallas kernels  36.9 us (91%)
  local copies, waits for them, and re-layouts  3.32 us (8%)
    pallas_call x1, Pallas kernels, local(): pl.pallas_call(functools.partial(kernel, n_blk, groups), out_shape=jax.Sh...  36.9 us
    unnamed x7, local copies, waits for them, and re-layouts  3.32 us

commit v1 on v0

v1 whole, which is shorter than its diff:
```python
import functools

import jax
import jax.numpy as jnp
from jax import lax
from jax.experimental import pallas as pl
from jax.experimental.pallas import tpu as pltpu
from jax.sharding import PartitionSpec as P

LANES = 128
CHUNK = 256
VMEM_BYTES = 67043328
E, G, Q, T, O = range(5)


def kernel(
    n_blk, groups, rk_ref, mk_ref, pay_ref, out_ref,
    pay, other_pay, mkeys, rkeys, hl, kcol, far, near, xr, yr_far, yr_near, zr,
    in_sem, key_send, key_recv, pair_send, pair_recv,
    x_send, x_recv, yf_send, yf_recv, yn_send, yn_recv, z_send, z_recv,
):
    blk = lax.axis_index("blk")
    rep = lax.axis_index("rep")
    group, core = rep // 2, rep % 2
    rows, width = pay.shape
    quarter = out_ref.shape[0]
    key_rows = mk_ref.shape[0]
    qrows = quarter // LANES
    chunk = min(CHUNK, quarter)
    n = quarter // chunk
    far_n = groups - 1

    side = 2 * (blk % 2) - 1
    at = lambda off: lax.rem(blk + off + n_blk, n_blk)
    block_of = {E: at(2 * side), G: at(-2 * side), Q: at(side), T: at(-side)}
    keys_to = {E: block_of[G], G: block_of[E], Q: block_of[Q], T: block_of[T]}
    mate = rep + 1 - 2 * core
    peers = [lax.rem(group + d, groups) * 2 + core for d in range(1, groups)]

    load_rk = pltpu.make_async_copy(rk_ref, rkeys.at[O], in_sem.at[0])
    load_mk = pltpu.make_async_copy(mk_ref, mkeys.at[pl.ds(0, key_rows)], in_sem.at[1])
    load_pay = pltpu.make_async_copy(pay_ref, pay, in_sem.at[2])
    for c in (load_rk, load_mk, load_pay):
        c.start()

    barrier = pltpu.get_barrier_semaphore()
    for i in (E, G, Q, T):
        pl.semaphore_signal(barrier, inc=1, device_id={"blk": block_of[i]})
    for r in peers + [mate]:
        pl.semaphore_signal(barrier, inc=1, device_id={"rep": r})
    load_rk.wait()
    load_mk.wait()
    pl.semaphore_wait(barrier, 5 + far_n)

    sent = []

    def send(src, dst, send_sem, recv_sem, to):
        c = pltpu.make_async_remote_copy(
            src_ref=src, dst_ref=dst, send_sem=send_sem, recv_sem=recv_sem, device_id=to)
        c.start()
        sent.append(c)
        return c

    keys = {}
    for i in (Q, E, G, T):
        keys[i] = send(rkeys.at[O], rkeys.at[i], key_send.at[i], key_recv.at[i], {"blk": keys_to[i]})
    pair_keys = send(
        mkeys.at[pl.ds(0, key_rows)], mkeys.at[pl.ds(key_rows, key_rows)], pair_send.at[0], pair_recv.at[0],
        {"rep": mate})
    pair_pay = send(pay_ref, other_pay, pair_send.at[1], pair_recv.at[1], {"rep": mate})

    def split(src, base):
        @pl.loop(0, rows // 256)
        def _(k):
            v = src[pl.ds(k * 256, 256), :]
            hi = v.astype(jnp.bfloat16)
            lo = (v - hi.astype(jnp.float32)).astype(jnp.bfloat16)
            hl[pl.ds(base + k * 256, 256), 0:width] = hi
            hl[pl.ds(base + k * 256, 256), width:2 * width] = lo

    def part(i, q, j, first, last):
        per = chunk // LANES
        for s in range(per):
            row = rkeys[i, pl.ds(q * qrows + j * per + s, 1), :]
            kcol[s * LANES:(s + 1) * LANES, :] = jnp.broadcast_to(row, (LANES, LANES)).T
        mine = kcol[...]
        hot = []
        for k in range(first // LANES, last // LANES):
            hot.append(jnp.where(mine == mkeys[k:k + 1, :], 1.0, 0.0).astype(jnp.bfloat16))
        both = jnp.dot(jnp.concatenate(hot, axis=1), hl[first:last, :], preferred_element_type=jnp.float32)
        return both[:, 0:width] + both[:, width:2 * width]

    def cut(j):
        return pl.ds(j * chunk, chunk)

    def compute_far(i, j, first=0, last=2 * rows, add=False):
        for d, r in enumerate(peers):
            v = part(i, r, j, first, last)
            far[i, d, cut(j), :] = far[i, d, cut(j), :] + v if add else v

    def compute_near(i, j, first=0, last=2 * rows, add=False):
        v = part(i, rep, j, first, last)
        near[i, cut(j), :] = near[i, cut(j), :] + v if add else v

    x_got, yf_got, yn_got, z_got = {}, {}, {}, {}
    x_slot, yf_slot, z_slot = {E: 0, G: 1, O: 2}, {Q: 0, T: 1}, {Q: 0, E: 1, G: 2}

    def send_x(i, j):
        s = x_slot[i]
        x_got[i, j] = [
            send(far.at[i, d, cut(j)], xr.at[s, d, cut(j)], x_send.at[s, d, j], x_recv.at[s, d, j], {"rep": r})
            for d, r in enumerate(peers)]

    def send_y_far(i, j):
        s = yf_slot[i]
        yf_got[i, j] = [
            send(far.at[i, d, cut(j)], yr_far.at[s, d, cut(j)], yf_send.at[s, d, j], yf_recv.at[s, d, j],
                 {"blk": block_of[T]})
            for d in range(far_n)]

    def send_y_near(j):
        yn_got[j] = send(
            near.at[T, cut(j)], yr_near.at[cut(j)], yn_send.at[j], yn_recv.at[j], {"blk": block_of[T]})

    def send_z(i, j):
        s = z_slot[i]
        z_got[i, j] = send(
            near.at[i, cut(j)], zr.at[s, cut(j)], z_send.at[s, j], z_recv.at[s, j],
            {"blk": block_of[G if i == G else E]})

    def join_far(i, src, j):
        for d in range(far_n):
            yf_got[src, j][d].wait_recv()
            far[i, d, cut(j), :] = far[i, d, cut(j), :] + yr_far[yf_slot[src], d, cut(j), :]

    def join_near(i, j):
        total = near[i, cut(j), :]
        for d in range(far_n):
            x_got[i, j][d].wait_recv()
            total = total + xr[x_slot[i], d, cut(j), :]
        near[i, cut(j), :] = total

    load_pay.wait()
    split(pay, 0)
    for j in range(n):
        compute_near(O, j, 0, rows)
    for j in range(n):
        compute_far(O, j, 0, rows)
    pair_keys.wait_recv()
    pair_pay.wait_recv()
    split(other_pay, rows)

    keys[Q].wait_recv()
    for j in range(n):
        compute_near(Q, j)
        send_z(Q, j)
        if j == 0:
            keys[E].wait_recv()
        compute_far(E, j)
        send_x(E, j)
        compute_far(Q, j)
        send_y_far(Q, j)
    keys[G].wait_recv()
    keys[T].wait_recv()
    for j in range(n):
        compute_near(E, j)
        compute_far(G, j)
        compute_far(T, j)
        send_y_far(T, j)
        join_near(E, j)
        send_z(E, j)
        join_far(G, Q, j)
        send_x(G, j)
    for j in range(n):
        compute_near(G, j)
        compute_far(O, j, rows, 2 * rows, add=True)
        compute_near(T, j)
        join_near(G, j)
        send_z(G, j)
        join_far(O, T, j)
        send_x(O, j)
        z_got[Q, j].wait_recv()
        near[T, cut(j), :] = near[T, cut(j), :] + zr[z_slot[Q], cut(j), :]
        send_y_near(j)
        compute_near(O, j, rows, 2 * rows, add=True)
    for j in range(n):
        z_got[E, j].wait_recv()
        near[O, cut(j), :] = near[O, cut(j), :] + zr[z_slot[E], cut(j), :]
    for j in range(n):
        join_near(O, j)
        yn_got[j].wait_recv()
        total = near[O, cut(j), :] + yr_near[cut(j), :]
        z_got[G, j].wait_recv()
        out_ref[cut(j), :] = total + zr[z_slot[G], cut(j), :]
    for c in sent:
        c.wait_send()


def solution(mesh):
    n_blk, n_rep = mesh.shape["blk"], mesh.shape["rep"]
    groups = n_rep // 2
    assert n_blk % 2 == 0 and n_blk > 5 and n_rep % 2 == 0, "odd mesh"

    def local(resident_keys, moving_keys, payload):
        res, rows, width = resident_keys.shape[0], payload.shape[0], payload.shape[1]
        quarter = res // n_rep
        far_n = groups - 1
        chunk = min(CHUNK, quarter)
        n = quarter // chunk
        f32, bf16, i32 = jnp.float32, jnp.bfloat16, jnp.int32
        dma = pltpu.SemaphoreType.DMA
        vmem = pl.BlockSpec(memory_space=pltpu.VMEM)
        hbm = pl.BlockSpec(memory_space=pltpu.HBM)
        return pl.pallas_call(
            functools.partial(kernel, n_blk, groups),
            out_shape=jax.ShapeDtypeStruct((quarter, width), f32),
            in_specs=[hbm, hbm, hbm],
            out_specs=vmem,
            scratch_shapes=[
                pltpu.VMEM((rows, width), f32),
                pltpu.VMEM((rows, width), f32),
                pltpu.VMEM((2 * rows // LANES, LANES), i32),
                pltpu.VMEM((5, res // LANES, LANES), i32),
                pltpu.VMEM((2 * rows, 2 * width), bf16),
                pltpu.VMEM((chunk, LANES), i32),
                pltpu.VMEM((5, far_n, quarter, width), f32),
                pltpu.VMEM((5, quarter, width), f32),
                pltpu.VMEM((3, far_n, quarter, width), f32),
                pltpu.VMEM((2, far_n, quarter, width), f32),
                pltpu.VMEM((quarter, width), f32),
                pltpu.VMEM((3, quarter, width), f32),
                dma((3,)),
                dma((4,)), dma((4,)),
                dma((2,)), dma((2,)),
                dma((3, far_n, n)), dma((3, far_n, n)),
                dma((2, far_n, n)), dma((2, far_n, n)),
                dma((n,)), dma((n,)),
                dma((3, n)), dma((3, n)),
            ],
            compiler_params=pltpu.CompilerParams(
                collective_id=0, has_side_effects=True, vmem_limit_bytes=VMEM_BYTES),
        )(resident_keys.reshape(res // LANES, LANES), moving_keys.reshape(rows // LANES, LANES), payload)

    in_specs = (P("blk"), P(("blk", "rep")), P(("blk", "rep"), None))
    out_specs = P(("blk", "rep"), None)
    return jax.shard_map(local, mesh=mesh, in_specs=in_specs, out_specs=out_specs, check_vma=False)
```

time: 40.5 us -> 36.2 us (0.89)
  Pallas kernels: 36.9 us -> 34.4 us
  local copies, waits for them, and re-layouts: 3.32 us -> 1.67 us
    pallas_call x1, Pallas kernels: 36.9 us -> 34.4 us  [local(): pl.pallas_call(functools.partial(kernel, n_blk, groups), out_shape=jax.Sh...]
    unnamed x7 -> x1, local copies, waits for them, and re-layouts: 3.32 us -> 1.67 us
where the time goes in v1:
time: 36.2 us; the launch traced here: 36 us
  Pallas kernels  34.4 us (95%)
  local copies, waits for them, and re-layouts  1.67 us (5%)
    pallas_call x1, Pallas kernels, local(): pl.pallas_call(functools.partial(kernel, n_blk, groups), out_shape=jax.Sh...  34.4 us
    unnamed x1, local copies, waits for them, and re-layouts  1.67 us

profile of v1, /device:TPU:0, one launch (start us, length us, event | category | flops | bytes accessed | tf_op | source)
XLA Modules:
  0.0 36.0 jit_solution(15418838155136915899)
XLA Ops:
  0.0 34.4 %shard_map.37 = f32[512,128]{1,0:T(8,128)} custom-call(s32[16,128]{1,0:T(8,128)} %bitcast.2, s32[16,128]{1,0:T(8,128)} %bitcast.3, f32[2048,128]{1,0:T(8,128)} %pay_ref.1), custom_call_target="tpu_custom_call" | custom-call | tf_op jit(solution)/shard_map/pallas_call | solution.py:214
  34.4 1.7 %copy.5 = f32[512,128]{1,0:T(8,128)} copy(f32[512,128]{1,0:T(8,128)} %shard_map.37) | data formatting | bytes 524288

commit v2 on v1

--- a/solution.py
+++ b/solution.py
@@ -9,7 +9,8 @@
 
 LANES = 128
 CHUNK = 256
-VMEM_BYTES = 67043328
+DEPTH = 1024
+VMEM_BYTES = 48 << 20
 E, G, Q, T, O = range(5)
 
 
@@ -83,12 +84,17 @@
         for s in range(per):
             row = rkeys[i, pl.ds(q * qrows + j * per + s, 1), :]
             kcol[s * LANES:(s + 1) * LANES, :] = jnp.broadcast_to(row, (LANES, LANES)).T
-        mine = kcol[...]
-        hot = []
-        for k in range(first // LANES, last // LANES):
-            hot.append(jnp.where(mine == mkeys[k:k + 1, :], 1.0, 0.0).astype(jnp.bfloat16))
-        both = jnp.dot(jnp.concatenate(hot, axis=1), hl[first:last, :], preferred_element_type=jnp.float32)
-        return both[:, 0:width] + both[:, width:2 * width]
+        total = None
+        for base in range(first, last, DEPTH):
+            mine = kcol[...]
+            hot = []
+            for k in range(base // LANES, (base + DEPTH) // LANES):
+                hot.append(jnp.where(mine == mkeys[k:k + 1, :], 1.0, 0.0).astype(jnp.bfloat16))
+            both = jnp.dot(
+                jnp.concatenate(hot, axis=1), hl[base:base + DEPTH, :], preferred_element_type=jnp.float32)
+            both = both[:, 0:width] + both[:, width:2 * width]
+            total = both if total is None else total + both
+        return total
 
     def cut(j):
         return pl.ds(j * chunk, chunk)
@@ -239,7 +245,8 @@
             ],
             compiler_params=pltpu.CompilerParams(
                 collective_id=0, has_side_effects=True, vmem_limit_bytes=VMEM_BYTES),
-        )(resident_keys.reshape(res // LANES, LANES), moving_keys.reshape(rows // LANES, LANES), payload)
+        )(*[pltpu.with_memory_space_constraint(v, pltpu.HBM) for v in (
+            resident_keys.reshape(res // LANES, LANES), moving_keys.reshape(rows // LANES, LANES), payload)])
 
     in_specs = (P("blk"), P(("blk", "rep")), P(("blk", "rep"), None))
     out_specs = P(("blk", "rep"), None)

time: 36.2 us -> 32.2 us (0.89)
  Pallas kernels: 34.4 us -> 31.3 us
  local copies, waits for them, and re-layouts: 1.67 us -> 0.71 us
    pallas_call x1, Pallas kernels: 34.4 us -> 31.3 us  [local(): pl.pallas_call(functools.partial(kernel, n_blk, groups), out_shape=jax.Sh...]
    unnamed x1, local copies, waits for them, and re-layouts: 1.67 us -> 0.71 us
where the time goes in v2:
time: 32.2 us; the launch traced here: 32.1 us
  Pallas kernels  31.3 us (97%)
  local copies, waits for them, and re-layouts  0.71 us (2%)
    pallas_call x1, Pallas kernels, local(): pl.pallas_call(functools.partial(kernel, n_blk, groups), out_shape=jax.Sh...  31.3 us
    unnamed x1, local copies, waits for them, and re-layouts  0.71 us

profile of v2, /device:TPU:0, one launch (start us, length us, event | category | flops | bytes accessed | tf_op | source)
XLA Modules:
  0.0 32.1 jit_solution(5205985598046869886)
XLA Ops:
  0.0 31.3 %shard_map.37 = f32[512,128]{1,0:T(8,128)S(1)} custom-call(s32[16,128]{1,0:T(8,128)} %bitcast.2, s32[16,128]{1,0:T(8,128)} %bitcast.3, f32[2048,128]{1,0:T(8,128)} %pay_ref.1), custom_call_target="tpu_custom_call" | custom-call | tf_op jit(solution)/shard_map/pallas_call | solution.py:220
  31.3 0.7 %copy.5 = f32[512,128]{1,0:T(8,128)} copy(f32[512,128]{1,0:T(8,128)S(1)} %shard_map.37) | data formatting | bytes 524288

commit v3 on v1

v3 whole, which is shorter than its diff:
```python
import functools

import jax
import jax.numpy as jnp
from jax import lax
from jax.experimental import pallas as pl
from jax.experimental.pallas import tpu as pltpu
from jax.sharding import PartitionSpec as P

LANES = 128
DEPTH = 1024
PIECES = 4
VMEM_BYTES = 48 << 20
U, D, Q, T, O = range(5)


def kernel(
    n_blk, groups, rk_ref, mk_ref, pay_ref, out_ref,
    pay, other_pay, mkeys, rkeys, hl, cols, part, xr, yr, zr_far, zr,
    in_sem, key_send, key_recv, pair_send, pair_recv,
    x_send, x_recv, yf_send, yf_recv, yn_send, yn_recv, zf_send, zf_recv, zn_send, zn_recv,
):
    blk = lax.axis_index("blk")
    rep = lax.axis_index("rep")
    group, core = rep // 2, rep % 2
    rows, width = pay.shape
    quarter = out_ref.shape[0]
    key_rows = mk_ref.shape[0]
    qrows = quarter // LANES
    piece = quarter // PIECES
    half = rows // 2
    far = range(1, groups)
    every = range(PIECES)

    odd = blk % 2
    side = 2 * odd - 1
    at = lambda off: lax.rem(blk + off + n_blk, n_blk)
    block_of = {U: at(2), D: at(-2), Q: at(side), T: at(-side)}
    F = (blk + n_blk - 2) // n_blk
    S = 1 - F
    keys_to = {U: block_of[D], D: block_of[U], Q: block_of[Q], T: block_of[T]}
    beside_q = at(2 * side)
    mate = rep + 1 - 2 * core
    owner = [rep] + [lax.rem(group + d, groups) * 2 + core for d in far]

    load_rk = pltpu.make_async_copy(rk_ref, rkeys.at[O], in_sem.at[0])
    load_mk = pltpu.make_async_copy(mk_ref, mkeys.at[pl.ds(0, key_rows)], in_sem.at[1])
    load_pay = pltpu.make_async_copy(pay_ref, pay, in_sem.at[2])
    for c in (load_rk, load_mk, load_pay):
        c.start()

    barrier = pltpu.get_barrier_semaphore()
    for i in (U, D, Q, T):
        pl.semaphore_signal(barrier, inc=1, device_id={"blk": block_of[i]})
    for r in owner[1:] + [mate]:
        pl.semaphore_signal(barrier, inc=1, device_id={"rep": r})

    sent = []

    def send(src, dst, send_sem, recv_sem, to):
        c = pltpu.make_async_remote_copy(
            src_ref=src, dst_ref=dst, send_sem=send_sem, recv_sem=recv_sem, device_id=to)
        c.start()
        sent.append(c)
        return c

    def columns(i, gs):
        for g in gs:
            for s in range(qrows):
                row = rkeys[i, pl.ds(owner[g] * qrows + s, 1), :]
                cols[i, g, s * LANES:(s + 1) * LANES, :] = jnp.broadcast_to(row, (LANES, LANES)).T

    def split(src, first, last, base):
        @pl.loop(first // 256, last // 256)
        def _(k):
            v = src[pl.ds(k * 256, 256), :]
            hi = v.astype(jnp.bfloat16)
            lo = (v - hi.astype(jnp.float32)).astype(jnp.bfloat16)
            hl[pl.ds(base + k * 256, 256), 0:width] = hi
            hl[pl.ds(base + k * 256, 256), width:2 * width] = lo

    def cut(p, count=1):
        return pl.ds(p * piece, count * piece)

    def compute(i, gs, p, count, first=0, last=2 * rows, add=False):
        for g in gs:
            total = part[i, g, cut(p, count), :] if add else None
            for base in range(first, last, DEPTH):
                mine = cols[i, g, cut(p, count), :]
                hot = []
                for k in range(base // LANES, (base + DEPTH) // LANES):
                    hot.append(jnp.where(mine == mkeys[k:k + 1, :], 1.0, 0.0).astype(jnp.bfloat16))
                both = jnp.dot(
                    jnp.concatenate(hot, axis=1), hl[base:base + DEPTH, :], preferred_element_type=jnp.float32)
                both = both[:, 0:width] + both[:, width:2 * width]
                total = both if total is None else total + both
            part[i, g, cut(p, count), :] = total

    near = range(1)
    x_got, yf_got, yn_got, zf_got = {}, {}, {}, {}

    def send_x(i, s, ps):
        for p in ps:
            x_got[s, p] = [
                send(part.at[i, d, cut(p)], xr.at[s, d - 1, cut(p)], x_send.at[s, d - 1, p], x_recv.at[s, d - 1, p],
                     {"rep": owner[d]})
                for d in far]

    def send_y_far(ps):
        for p in ps:
            yf_got[p] = [
                send(part.at[T, d, cut(p)], yr.at[1 + d, cut(p)], yf_send.at[d - 1, p], yf_recv.at[d - 1, p],
                     {"blk": block_of[T]})
                for d in far]

    def send_y_near(i, ps):
        s = {Q: 0, T: 1}[i]
        for p in ps:
            yn_got[i, p] = send(
                part.at[i, 0, cut(p)], yr.at[s, cut(p)], yn_send.at[s, p], yn_recv.at[s, p], {"blk": block_of[T]})

    def send_z_far(ps):
        for p in ps:
            zf_got[p] = [
                send(part.at[Q, d, cut(p)], zr_far.at[d - 1, cut(p)], zf_send.at[d - 1, p], zf_recv.at[d - 1, p],
                     {"blk": beside_q})
                for d in far]

    def z_near(i, p):
        return pltpu.make_async_remote_copy(
            src_ref=part.at[i, 0, cut(p)], dst_ref=zr.at[i, cut(p)], send_sem=zn_send.at[i, p],
            recv_sem=zn_recv.at[i, p], device_id={"blk": at(2 - 4 * i)})

    def join_z_near(i, s, ps):
        keep = i == odd
        for p in ps:
            total = part[i, 0, cut(p), :]
            for c in x_got[s, p]:
                c.wait_recv()
            if s == 0:
                yn_got[Q, p].wait_recv()
            for d in far:
                total = total + xr[s, d - 1, cut(p), :]
            part[i, 0, cut(p), :] = total + jnp.where(keep, yr[0, cut(p), :], 0.0)
            c = z_near(i, p)
            c.start()
            sent.append(c)

    def join_y_far(ps):
        for p in ps:
            for d in far:
                zf_got[p][d - 1].wait_recv()
                part[T, d, cut(p), :] = part[T, d, cut(p), :] + zr_far[d - 1, cut(p), :]
            send_y_far([p])

    def join_x_own(ps):
        for p in ps:
            for d in far:
                yf_got[p][d - 1].wait_recv()
                part[O, d, cut(p), :] = part[O, d, cut(p), :] + yr[1 + d, cut(p), :]
            send_x(O, 2, [p])

    load_rk.wait()
    load_mk.wait()
    pl.semaphore_wait(barrier, 4 + groups)
    for i in (Q, U, D, T):
        send(rkeys.at[O], rkeys.at[i], key_send.at[i], key_recv.at[i], {"blk": keys_to[i]})

    def keys_of(i):
        pltpu.make_async_remote_copy(
            src_ref=rkeys.at[O], dst_ref=rkeys.at[i], send_sem=key_send.at[i], recv_sem=key_recv.at[i],
            device_id={"blk": block_of[T]}).wait_recv()

    pair = [send(
        mkeys.at[pl.ds(0, key_rows)], mkeys.at[pl.ds(key_rows, key_rows)], pair_send.at[0], pair_recv.at[0],
        {"rep": mate})]
    for h in range(2):
        pair.append(send(
            pay_ref.at[pl.ds(h * half, half)], other_pay.at[pl.ds(h * half, half)], pair_send.at[1 + h],
            pair_recv.at[1 + h], {"rep": mate}))
    both = range(groups)
    columns(O, both)
    load_pay.wait()
    split(pay, 0, rows, 0)
    compute(O, both, 0, PIECES, 0, rows)
    pair[0].wait_recv()
    pair[1].wait_recv()
    split(other_pay, 0, half, rows)
    keys_of(F)
    columns(F, far)
    pair[2].wait_recv()
    split(other_pay, half, rows, rows)

    a, b, c, d = every
    compute(F, far, a, 2)
    send_x(F, 0, (a, b))
    keys_of(Q)
    columns(Q, both)
    compute(Q, far, a, 1)
    compute(Q, near, a, 1)
    send_z_far([a])
    send_y_near(Q, [a])
    compute(Q, far, b, 1)
    compute(Q, near, b, 1)
    compute(F, far, c, 1)
    columns(F, near)
    send_z_far([b])
    send_y_near(Q, [b])
    send_x(F, 0, [c])
    keys_of(S)
    compute(F, far, d, 1)
    compute(Q, far, c, 2)
    compute(Q, near, c, 2)
    columns(S, both)
    send_x(F, 0, [d])
    send_z_far((c, d))
    send_y_near(Q, (c, d))
    keys_of(T)
    compute(S, far, a, 2)
    compute(F, near, a, 2)
    columns(T, both)
    send_x(S, 1, (a, b))
    join_z_near(F, 0, [a])
    compute(T, far, a, 2)
    compute(S, far, c, 2)
    send_x(S, 1, (c, d))
    join_z_near(F, 0, [b])
    join_y_far([a])
    compute(F, near, c, 2)
    compute(T, far, c, 2)
    join_z_near(F, 0, [c])
    join_y_far([b])
    compute(O, far, a, PIECES, rows, 2 * rows, add=True)
    join_z_near(F, 0, [d])
    join_y_far([c])
    compute(S, near, a, PIECES)
    join_z_near(S, 1, [a])
    join_y_far([d])
    compute(T, near, a, PIECES)
    send_y_near(T, every)
    join_x_own([a])
    join_z_near(S, 1, [b])
    compute(O, near, a, PIECES, rows, 2 * rows, add=True)
    join_x_own([b])
    join_z_near(S, 1, [c])
    join_x_own([c])
    join_z_near(S, 1, [d])
    join_x_own([d])
    for p in every:
        z_near(D, p).wait_recv()
        part[O, 0, cut(p), :] = part[O, 0, cut(p), :] + zr[D, cut(p), :]
    for p in every:
        total = part[O, 0, cut(p), :]
        for c in x_got[2, p]:
            c.wait_recv()
        yn_got[T, p].wait_recv()
        for d in far:
            total = total + xr[2, d - 1, cut(p), :]
        total = total + yr[1, cut(p), :]
        z_near(U, p).wait_recv()
        out_ref[cut(p), :] = total + zr[U, cut(p), :]
    for c in sent:
        c.wait_send()


def solution(mesh):
    n_blk, n_rep = mesh.shape["blk"], mesh.shape["rep"]
    groups = n_rep // 2
    assert n_blk % 2 == 0 and n_blk > 5 and n_rep % 2 == 0, "odd mesh"

    def local(resident_keys, moving_keys, payload):
        res, rows, width = resident_keys.shape[0], payload.shape[0], payload.shape[1]
        quarter = res // n_rep
        far_n = groups - 1
        f32, bf16, i32 = jnp.float32, jnp.bfloat16, jnp.int32
        dma = pltpu.SemaphoreType.DMA
        vmem = pl.BlockSpec(memory_space=pltpu.VMEM)
        hbm = pl.BlockSpec(memory_space=pltpu.HBM)
        operands = (resident_keys.reshape(res // LANES, LANES), moving_keys.reshape(rows // LANES, LANES), payload)
        return pl.pallas_call(
            functools.partial(kernel, n_blk, groups),
            out_shape=jax.ShapeDtypeStruct((quarter, width), f32),
            in_specs=[hbm, hbm, hbm],
            out_specs=vmem,
            scratch_shapes=[
                pltpu.VMEM((rows, width), f32),
                pltpu.VMEM((rows, width), f32),
                pltpu.VMEM((2 * rows // LANES, LANES), i32),
                pltpu.VMEM((5, res // LANES, LANES), i32),
                pltpu.VMEM((2 * rows, 2 * width), bf16),
                pltpu.VMEM((5, groups, quarter, LANES), i32),
                pltpu.VMEM((5, groups, quarter, width), f32),
                pltpu.VMEM((3, far_n, quarter, width), f32),
                pltpu.VMEM((2 + far_n, quarter, width), f32),
                pltpu.VMEM((far_n, quarter, width), f32),
                pltpu.VMEM((2, quarter, width), f32),
                dma((3,)),
                dma((4,)), dma((4,)),
                dma((3,)), dma((3,)),
                dma((3, far_n, PIECES)), dma((3, far_n, PIECES)),
                dma((far_n, PIECES)), dma((far_n, PIECES)),
                dma((2, PIECES)), dma((2, PIECES)),
                dma((far_n, PIECES)), dma((far_n, PIECES)),
                dma((2, PIECES)), dma((2, PIECES)),
            ],
            compiler_params=pltpu.CompilerParams(
                collective_id=0, has_side_effects=True, vmem_limit_bytes=VMEM_BYTES),
        )(*[pltpu.with_memory_space_constraint(v, pltpu.HBM) for v in operands])

    in_specs = (P("blk"), P(("blk", "rep")), P(("blk", "rep"), None))
    out_specs = P(("blk", "rep"), None)
    return jax.shard_map(local, mesh=mesh, in_specs=in_specs, out_specs=out_specs, check_vma=False)
```

time: 36.2 us -> 30.8 us (0.85)
  Pallas kernels: 34.4 us -> 29.6 us
  local copies, waits for them, and re-layouts: 1.67 us -> 0.71 us
    pallas_call x1, Pallas kernels: 34.4 us -> 29.6 us  [local(): pl.pallas_call(functools.partial(kernel, n_blk, groups), out_shape=jax.Sh...]
    unnamed x1, local copies, waits for them, and re-layouts: 1.67 us -> 0.71 us
where the time goes in v3:
time: 30.8 us; the launch traced here: 30.3 us
  Pallas kernels  29.6 us (96%)
  local copies, waits for them, and re-layouts  0.71 us (2%)
    pallas_call x1, Pallas kernels, local(): pl.pallas_call(functools.partial(kernel, n_blk, groups), out_shape=jax.Sh...  29.6 us
    unnamed x1, local copies, waits for them, and re-layouts  0.71 us

profile of v3, /device:TPU:0, one launch (start us, length us, event | category | flops | bytes accessed | tf_op | source)
XLA Modules:
  0.0 30.3 jit_solution(3229200614430481829)
XLA Ops:
  0.0 29.6 %shard_map.37 = f32[512,128]{1,0:T(8,128)S(1)} custom-call(s32[16,128]{1,0:T(8,128)} %bitcast.2, s32[16,128]{1,0:T(8,128)} %bitcast.3, f32[2048,128]{1,0:T(8,128)} %pay_ref.1), custom_call_target="tpu_custom_call" | custom-call | tf_op jit(solution)/shard_map/pallas_call | solution.py:280
  29.6 0.7 %copy.5 = f32[512,128]{1,0:T(8,128)} copy(f32[512,128]{1,0:T(8,128)S(1)} %shard_map.37) | data formatting | bytes 524288

commit v4 on v3

--- a/solution.py
+++ b/solution.py
@@ -17,8 +17,8 @@
 def kernel(
     n_blk, groups, rk_ref, mk_ref, pay_ref, out_ref,
     pay, other_pay, mkeys, rkeys, hl, cols, part, xr, yr, zr_far, zr,
-    in_sem, key_send, key_recv, pair_send, pair_recv,
-    x_send, x_recv, yf_send, yf_recv, yn_send, yn_recv, zf_send, zf_recv, zn_send, zn_recv,
+    in_sem, sends, key_recv, pair_recv,
+    x_recv, yf_recv, yn_recv, zf_recv, zn_recv,
 ):
     blk = lax.axis_index("blk")
     rep = lax.axis_index("rep")
@@ -36,7 +36,7 @@
     side = 2 * odd - 1
     at = lambda off: lax.rem(blk + off + n_blk, n_blk)
     block_of = {U: at(2), D: at(-2), Q: at(side), T: at(-side)}
-    F = (blk + n_blk - 2) // n_blk
+    F = (2 * blk) // n_blk
     S = 1 - F
     keys_to = {U: block_of[D], D: block_of[U], Q: block_of[Q], T: block_of[T]}
     beside_q = at(2 * side)
@@ -55,13 +55,13 @@
     for r in owner[1:] + [mate]:
         pl.semaphore_signal(barrier, inc=1, device_id={"rep": r})
 
-    sent = []
-
-    def send(src, dst, send_sem, recv_sem, to):
+    classes = [xr, yr, zr_far, zr, rkeys.at[pl.ds(0, 4)], mkeys.at[pl.ds(0, key_rows)], pay]
+    BY_X, BY_Y, BY_Z_FAR, BY_Z, KEYS, PAIR_KEYS, PAIR = range(len(classes))
+
+    def send(src, dst, kind, recv_sem, to):
         c = pltpu.make_async_remote_copy(
-            src_ref=src, dst_ref=dst, send_sem=send_sem, recv_sem=recv_sem, device_id=to)
+            src_ref=src, dst_ref=dst, send_sem=sends.at[kind], recv_sem=recv_sem, device_id=to)
         c.start()
-        sent.append(c)
         return c
 
     def columns(i, gs):
@@ -102,14 +102,14 @@
     def send_x(i, s, ps):
         for p in ps:
             x_got[s, p] = [
-                send(part.at[i, d, cut(p)], xr.at[s, d - 1, cut(p)], x_send.at[s, d - 1, p], x_recv.at[s, d - 1, p],
+                send(part.at[i, d, cut(p)], xr.at[s, d - 1, cut(p)], BY_X, x_recv.at[s, d - 1, p],
                      {"rep": owner[d]})
                 for d in far]
 
     def send_y_far(ps):
         for p in ps:
             yf_got[p] = [
-                send(part.at[T, d, cut(p)], yr.at[1 + d, cut(p)], yf_send.at[d - 1, p], yf_recv.at[d - 1, p],
+                send(part.at[T, d, cut(p)], yr.at[1 + d, cut(p)], BY_Y, yf_recv.at[d - 1, p],
                      {"blk": block_of[T]})
                 for d in far]
 
@@ -117,19 +117,14 @@
         s = {Q: 0, T: 1}[i]
         for p in ps:
             yn_got[i, p] = send(
-                part.at[i, 0, cut(p)], yr.at[s, cut(p)], yn_send.at[s, p], yn_recv.at[s, p], {"blk": block_of[T]})
+                part.at[i, 0, cut(p)], yr.at[s, cut(p)], BY_Y, yn_recv.at[s, p], {"blk": block_of[T]})
 
     def send_z_far(ps):
         for p in ps:
             zf_got[p] = [
-                send(part.at[Q, d, cut(p)], zr_far.at[d - 1, cut(p)], zf_send.at[d - 1, p], zf_recv.at[d - 1, p],
+                send(part.at[Q, d, cut(p)], zr_far.at[d - 1, cut(p)], BY_Z_FAR, zf_recv.at[d - 1, p],
                      {"blk": beside_q})
                 for d in far]
-
-    def z_near(i, p):
-        return pltpu.make_async_remote_copy(
-            src_ref=part.at[i, 0, cut(p)], dst_ref=zr.at[i, cut(p)], send_sem=zn_send.at[i, p],
-            recv_sem=zn_recv.at[i, p], device_id={"blk": at(2 - 4 * i)})
 
     def join_z_near(i, s, ps):
         keep = i == odd
@@ -137,14 +132,12 @@
             total = part[i, 0, cut(p), :]
             for c in x_got[s, p]:
                 c.wait_recv()
-            if s == 0:
-                yn_got[Q, p].wait_recv()
+            if (Q, p) in yn_got:
+                yn_got.pop((Q, p)).wait_recv()
             for d in far:
                 total = total + xr[s, d - 1, cut(p), :]
             part[i, 0, cut(p), :] = total + jnp.where(keep, yr[0, cut(p), :], 0.0)
-            c = z_near(i, p)
-            c.start()
-            sent.append(c)
+            send(part.at[i, 0, cut(p)], zr.at[i, cut(p)], BY_Z, zn_recv.at[i], {"blk": at(2 - 4 * i)})
 
     def join_y_far(ps):
         for p in ps:
@@ -160,26 +153,26 @@
                 part[O, d, cut(p), :] = part[O, d, cut(p), :] + yr[1 + d, cut(p), :]
             send_x(O, 2, [p])
 
+    both = range(groups)
     load_rk.wait()
     load_mk.wait()
+    columns(O, both)
     pl.semaphore_wait(barrier, 4 + groups)
     for i in (Q, U, D, T):
-        send(rkeys.at[O], rkeys.at[i], key_send.at[i], key_recv.at[i], {"blk": keys_to[i]})
+        send(rkeys.at[O], rkeys.at[i], KEYS, key_recv.at[i], {"blk": keys_to[i]})
 
     def keys_of(i):
         pltpu.make_async_remote_copy(
-            src_ref=rkeys.at[O], dst_ref=rkeys.at[i], send_sem=key_send.at[i], recv_sem=key_recv.at[i],
+            src_ref=rkeys.at[O], dst_ref=rkeys.at[i], send_sem=sends.at[KEYS], recv_sem=key_recv.at[i],
             device_id={"blk": block_of[T]}).wait_recv()
 
     pair = [send(
-        mkeys.at[pl.ds(0, key_rows)], mkeys.at[pl.ds(key_rows, key_rows)], pair_send.at[0], pair_recv.at[0],
+        mkeys.at[pl.ds(0, key_rows)], mkeys.at[pl.ds(key_rows, key_rows)], PAIR_KEYS, pair_recv.at[0],
         {"rep": mate})]
     for h in range(2):
         pair.append(send(
-            pay_ref.at[pl.ds(h * half, half)], other_pay.at[pl.ds(h * half, half)], pair_send.at[1 + h],
-            pair_recv.at[1 + h], {"rep": mate}))
-    both = range(groups)
-    columns(O, both)
+            pay_ref.at[pl.ds(h * half, half)], other_pay.at[pl.ds(h * half, half)], PAIR, pair_recv.at[1 + h],
+            {"rep": mate}))
     load_pay.wait()
     split(pay, 0, rows, 0)
     compute(O, both, 0, PIECES, 0, rows)
@@ -192,8 +185,14 @@
     split(other_pay, half, rows, rows)
 
     a, b, c, d = every
-    compute(F, far, a, 2)
-    send_x(F, 0, (a, b))
+    compute(F, far, a, 1)
+    send_x(F, 0, [a])
+    keys_of(T)
+    columns(T, near)
+    compute(F, far, b, 1)
+    compute(T, near, a, 1)
+    send_x(F, 0, [b])
+    send_y_near(T, [a])
     keys_of(Q)
     columns(Q, both)
     compute(Q, far, a, 1)
@@ -202,65 +201,71 @@
     send_y_near(Q, [a])
     compute(Q, far, b, 1)
     compute(Q, near, b, 1)
-    compute(F, far, c, 1)
     columns(F, near)
     send_z_far([b])
     send_y_near(Q, [b])
-    send_x(F, 0, [c])
     keys_of(S)
-    compute(F, far, d, 1)
-    compute(Q, far, c, 2)
-    compute(Q, near, c, 2)
-    columns(S, both)
-    send_x(F, 0, [d])
-    send_z_far((c, d))
-    send_y_near(Q, (c, d))
-    keys_of(T)
-    compute(S, far, a, 2)
-    compute(F, near, a, 2)
-    columns(T, both)
-    send_x(S, 1, (a, b))
+    columns(S, far)
+    compute(S, far, a, 1)
+    compute(Q, far, c, 1)
+    compute(Q, near, c, 1)
+    send_x(S, 1, [a])
+    send_z_far([c])
+    send_y_near(Q, [c])
+    compute(S, far, b, 1)
+    compute(Q, far, d, 1)
+    compute(Q, near, d, 1)
+    compute(F, near, a, 1)
+    columns(S, near)
+    send_x(S, 1, [b])
+    send_z_far([d])
+    send_y_near(Q, [d])
+    compute(S, far, c, 2)
+    compute(F, near, b, 1)
+    columns(T, far)
+    send_x(S, 1, (c, d))
     join_z_near(F, 0, [a])
+    compute(S, near, a, 2)
     compute(T, far, a, 2)
-    compute(S, far, c, 2)
-    send_x(S, 1, (c, d))
     join_z_near(F, 0, [b])
+    join_z_near(S, 1, [a])
     join_y_far([a])
+    compute(F, far, c, 2)
+    compute(T, far, c, 2)
+    send_x(F, 0, (c, d))
+    join_z_near(S, 1, [b])
+    join_y_far([b])
+    compute(S, near, c, 2)
     compute(F, near, c, 2)
-    compute(T, far, c, 2)
-    join_z_near(F, 0, [c])
-    join_y_far([b])
+    join_z_near(S, 1, [c])
+    join_y_far([c])
     compute(O, far, a, PIECES, rows, 2 * rows, add=True)
-    join_z_near(F, 0, [d])
-    join_y_far([c])
-    compute(S, near, a, PIECES)
-    join_z_near(S, 1, [a])
+    join_x_own([a])
+    join_z_near(S, 1, [d])
     join_y_far([d])
-    compute(T, near, a, PIECES)
-    send_y_near(T, every)
-    join_x_own([a])
-    join_z_near(S, 1, [b])
+    compute(T, near, b, PIECES - 1)
+    send_y_near(T, (b, c, d))
+    join_x_own([b])
     compute(O, near, a, PIECES, rows, 2 * rows, add=True)
-    join_x_own([b])
-    join_z_near(S, 1, [c])
-    join_x_own([c])
-    join_z_near(S, 1, [d])
-    join_x_own([d])
+    for p in (c, d):
+        join_z_near(F, 0, [p])
+        join_x_own([p])
+    for i in (D, U):
+        pltpu.make_async_remote_copy(
+            src_ref=part.at[i, 0], dst_ref=zr.at[i], send_sem=sends.at[BY_Z], recv_sem=zn_recv.at[i],
+            device_id={"blk": block_of[i]}).wait_recv()
     for p in every:
-        z_near(D, p).wait_recv()
-        part[O, 0, cut(p), :] = part[O, 0, cut(p), :] + zr[D, cut(p), :]
-    for p in every:
-        total = part[O, 0, cut(p), :]
+        total = part[O, 0, cut(p), :] + zr[D, cut(p), :] + zr[U, cut(p), :]
         for c in x_got[2, p]:
             c.wait_recv()
-        yn_got[T, p].wait_recv()
         for d in far:
             total = total + xr[2, d - 1, cut(p), :]
-        total = total + yr[1, cut(p), :]
-        z_near(U, p).wait_recv()
-        out_ref[cut(p), :] = total + zr[U, cut(p), :]
-    for c in sent:
-        c.wait_send()
+        yn_got[T, p].wait_recv()
+        out_ref[cut(p), :] = total + yr[1, cut(p), :]
+    for kind, ref in enumerate(classes):
+        pltpu.make_async_remote_copy(
+            src_ref=ref, dst_ref=ref, send_sem=sends.at[kind], recv_sem=pair_recv.at[0],
+            device_id={"rep": mate}).wait_send()
 
 
 def solution(mesh):
@@ -295,13 +300,14 @@
                 pltpu.VMEM((far_n, quarter, width), f32),
                 pltpu.VMEM((2, quarter, width), f32),
                 dma((3,)),
-                dma((4,)), dma((4,)),
-                dma((3,)), dma((3,)),
-                dma((3, far_n, PIECES)), dma((3, far_n, PIECES)),
-                dma((far_n, PIECES)), dma((far_n, PIECES)),
-                dma((2, PIECES)), dma((2, PIECES)),
-                dma((far_n, PIECES)), dma((far_n, PIECES)),
-                dma((2, PIECES)), dma((2, PIECES)),
+                dma((7,)),
+                dma((4,)),
+                dma((3,)),
+                dma((3, far_n, PIECES)),
+                dma((far_n, PIECES)),
+                dma((2, PIECES)),
+                dma((far_n, PIECES)),
+                dma((2,)),
             ],
             compiler_params=pltpu.CompilerParams(
                 collective_id=0, has_side_effects=True, vmem_limit_bytes=VMEM_BYTES),

time: 30.8 us -> 30.3 us (0.984)
  no operation moved by 1% of the time
where the time goes in v4:
time: 30.3 us; the launch traced here: 30.1 us
  Pallas kernels  29.4 us (97%)
  local copies, waits for them, and re-layouts  0.71 us (2%)
    pallas_call x1, Pallas kernels, local(): pl.pallas_call(functools.partial(kernel, n_blk, groups), out_shape=jax.Sh...  29.4 us
    unnamed x1, local copies, waits for them, and re-layouts  0.71 us

profile of v4, /device:TPU:0, one launch (start us, length us, event | category | flops | bytes accessed | tf_op | source)
XLA Modules:
  0.0 30.1 jit_solution(6781846555789299044)
XLA Ops:
  0.0 29.4 %shard_map.37 = f32[512,128]{1,0:T(8,128)S(1)} custom-call(s32[16,128]{1,0:T(8,128)} %bitcast.2, s32[16,128]{1,0:T(8,128)} %bitcast.3, f32[2048,128]{1,0:T(8,128)} %pay_ref.1), custom_call_target="tpu_custom_call" | custom-call | tf_op jit(solution)/shard_map/pallas_call | solution.py:285
  29.4 0.7 %copy.5 = f32[512,128]{1,0:T(8,128)} copy(f32[512,128]{1,0:T(8,128)S(1)} %shard_map.37) | data formatting | bytes 524288

commit v5 on v4

--- a/solution.py
+++ b/solution.py
@@ -187,18 +187,14 @@
     a, b, c, d = every
     compute(F, far, a, 1)
     send_x(F, 0, [a])
-    keys_of(T)
-    columns(T, near)
-    compute(F, far, b, 1)
-    compute(T, near, a, 1)
-    send_x(F, 0, [b])
-    send_y_near(T, [a])
     keys_of(Q)
     columns(Q, both)
+    compute(F, far, b, 1)
     compute(Q, far, a, 1)
     compute(Q, near, a, 1)
     send_z_far([a])
     send_y_near(Q, [a])
+    send_x(F, 0, [b])
     compute(Q, far, b, 1)
     compute(Q, near, b, 1)
     columns(F, near)
@@ -220,10 +216,13 @@
     send_x(S, 1, [b])
     send_z_far([d])
     send_y_near(Q, [d])
+    keys_of(T)
     compute(S, far, c, 2)
     compute(F, near, b, 1)
-    columns(T, far)
+    columns(T, both)
+    compute(T, near, a, 1)
     send_x(S, 1, (c, d))
+    send_y_near(T, [a])
     join_z_near(F, 0, [a])
     compute(S, near, a, 2)
     compute(T, far, a, 2)
@@ -236,15 +235,15 @@
     join_z_near(S, 1, [b])
     join_y_far([b])
     compute(S, near, c, 2)
-    compute(F, near, c, 2)
+    compute(T, near, b, PIECES - 1)
     join_z_near(S, 1, [c])
     join_y_far([c])
     compute(O, far, a, PIECES, rows, 2 * rows, add=True)
+    join_y_far([d])
+    send_y_near(T, (b, c, d))
     join_x_own([a])
     join_z_near(S, 1, [d])
-    join_y_far([d])
-    compute(T, near, b, PIECES - 1)
-    send_y_near(T, (b, c, d))
+    compute(F, near, c, 2)
     join_x_own([b])
     compute(O, near, a, PIECES, rows, 2 * rows, add=True)
     for p in (c, d):

time: 30.3 us -> 29.9 us (0.987)
  Pallas kernels: 29.4 us -> 29 us
    pallas_call x1, Pallas kernels: 29.4 us -> 29 us  [local(): pl.pallas_call(functools.partial(kernel, n_blk, groups), out_shape=jax.Sh...]
where the time goes in v5:
time: 29.9 us; the launch traced here: 29.8 us
  Pallas kernels  29 us (97%)
  local copies, waits for them, and re-layouts  0.71 us (2%)
    pallas_call x1, Pallas kernels, local(): pl.pallas_call(functools.partial(kernel, n_blk, groups), out_shape=jax.Sh...  29 us
    unnamed x1, local copies, waits for them, and re-layouts  0.71 us

profile of v5, /device:TPU:0, one launch (start us, length us, event | category | flops | bytes accessed | tf_op | source)
XLA Modules:
  0.0 29.8 jit_solution(743024097221198709)
XLA Ops:
  0.0 29.0 %shard_map.37 = f32[512,128]{1,0:T(8,128)S(1)} custom-call(s32[16,128]{1,0:T(8,128)} %bitcast.2, s32[16,128]{1,0:T(8,128)} %bitcast.3, f32[2048,128]{1,0:T(8,128)} %pay_ref.1), custom_call_target="tpu_custom_call" | custom-call | tf_op jit(solution)/shard_map/pallas_call | solution.py:284
  29.0 0.7 %copy.5 = f32[512,128]{1,0:T(8,128)} copy(f32[512,128]{1,0:T(8,128)S(1)} %shard_map.37) | data formatting | bytes 524288

commit v6 on v5

--- a/solution.py
+++ b/solution.py
@@ -55,8 +55,8 @@
     for r in owner[1:] + [mate]:
         pl.semaphore_signal(barrier, inc=1, device_id={"rep": r})
 
-    classes = [xr, yr, zr_far, zr, rkeys.at[pl.ds(0, 4)], mkeys.at[pl.ds(0, key_rows)], pay]
-    BY_X, BY_Y, BY_Z_FAR, BY_Z, KEYS, PAIR_KEYS, PAIR = range(len(classes))
+    classes = [xr, yr, yr, rkeys.at[pl.ds(0, 4)], mkeys.at[pl.ds(0, key_rows)], pay]
+    BY_X, BY_Y, BY_Z, KEYS, PAIR_KEYS, PAIR = range(len(classes))
 
     def send(src, dst, kind, recv_sem, to):
         c = pltpu.make_async_remote_copy(
@@ -122,7 +122,7 @@
     def send_z_far(ps):
         for p in ps:
             zf_got[p] = [
-                send(part.at[Q, d, cut(p)], zr_far.at[d - 1, cut(p)], BY_Z_FAR, zf_recv.at[d - 1, p],
+                send(part.at[Q, d, cut(p)], zr_far.at[d - 1, cut(p)], BY_Z, zf_recv.at[d - 1, p],
                      {"blk": beside_q})
                 for d in far]
 
@@ -185,16 +185,14 @@
     split(other_pay, half, rows, rows)
 
     a, b, c, d = every
-    compute(F, far, a, 1)
-    send_x(F, 0, [a])
+    compute(F, far, a, 2)
+    send_x(F, 0, (a, b))
     keys_of(Q)
     columns(Q, both)
-    compute(F, far, b, 1)
     compute(Q, far, a, 1)
     compute(Q, near, a, 1)
     send_z_far([a])
     send_y_near(Q, [a])
-    send_x(F, 0, [b])
     compute(Q, far, b, 1)
     compute(Q, near, b, 1)
     columns(F, near)
@@ -299,7 +297,7 @@
                 pltpu.VMEM((far_n, quarter, width), f32),
                 pltpu.VMEM((2, quarter, width), f32),
                 dma((3,)),
-                dma((7,)),
+                dma((6,)),
                 dma((4,)),
                 dma((3,)),
                 dma((3, far_n, PIECES)),

time: 29.9 us -> 29.8 us (level)
  no operation moved by 1% of the time
where the time goes in v6:
time: 29.8 us; the launch traced here: 29.6 us
  Pallas kernels  28.9 us (97%)
  local copies, waits for them, and re-layouts  0.71 us (2%)
    pallas_call x1, Pallas kernels, local(): pl.pallas_call(functools.partial(kernel, n_blk, groups), out_shape=jax.Sh...  28.9 us
    unnamed x1, local copies, waits for them, and re-layouts  0.71 us

profile of v6, /device:TPU:0, one launch (start us, length us, event | category | flops | bytes accessed | tf_op | source)
XLA Modules:
  0.0 29.6 jit_solution(6000500273675119567)
XLA Ops:
  0.0 28.9 %shard_map.37 = f32[512,128]{1,0:T(8,128)S(1)} custom-call(s32[16,128]{1,0:T(8,128)} %bitcast.2, s32[16,128]{1,0:T(8,128)} %bitcast.3, f32[2048,128]{1,0:T(8,128)} %pay_ref.1), custom_call_target="tpu_custom_call" | custom-call | tf_op jit(solution)/shard_map/pallas_call | solution.py:282
  28.9 0.7 %copy.5 = f32[512,128]{1,0:T(8,128)} copy(f32[512,128]{1,0:T(8,128)S(1)} %shard_map.37) | data formatting | bytes 524288

commit v7 on v6

--- a/solution.py
+++ b/solution.py
@@ -175,7 +175,7 @@
             {"rep": mate}))
     load_pay.wait()
     split(pay, 0, rows, 0)
-    compute(O, both, 0, PIECES, 0, rows)
+    compute(O, near, 0, PIECES, 0, rows)
     pair[0].wait_recv()
     pair[1].wait_recv()
     split(other_pay, 0, half, rows)
@@ -236,7 +236,7 @@
     compute(T, near, b, PIECES - 1)
     join_z_near(S, 1, [c])
     join_y_far([c])
-    compute(O, far, a, PIECES, rows, 2 * rows, add=True)
+    compute(O, far, a, PIECES)
     join_y_far([d])
     send_y_near(T, (b, c, d))
     join_x_own([a])

time: 29.8 us -> 29.8 us (level)
  no operation moved by 1% of the time
where the time goes in v7:
time: 29.8 us; the launch traced here: 29.6 us
  Pallas kernels  28.9 us (97%)
  local copies, waits for them, and re-layouts  0.71 us (2%)
    pallas_call x1, Pallas kernels, local(): pl.pallas_call(functools.partial(kernel, n_blk, groups), out_shape=jax.Sh...  28.9 us
    unnamed x1, local copies, waits for them, and re-layouts  0.71 us

profile of v7, /device:TPU:0, one launch (start us, length us, event | category | flops | bytes accessed | tf_op | source)
XLA Modules:
  0.0 29.6 jit_solution(510676791965857273)
XLA Ops:
  0.0 28.9 %shard_map.37 = f32[512,128]{1,0:T(8,128)S(1)} custom-call(s32[16,128]{1,0:T(8,128)} %bitcast.2, s32[16,128]{1,0:T(8,128)} %bitcast.3, f32[2048,128]{1,0:T(8,128)} %pay_ref.1), custom_call_target="tpu_custom_call" | custom-call | tf_op jit(solution)/shard_map/pallas_call | solution.py:282
  28.9 0.7 %copy.5 = f32[512,128]{1,0:T(8,128)} copy(f32[512,128]{1,0:T(8,128)S(1)} %shard_map.37) | data formatting | bytes 524288

commit v8 on v6

--- a/solution.py
+++ b/solution.py
@@ -137,7 +137,7 @@
             for d in far:
                 total = total + xr[s, d - 1, cut(p), :]
             part[i, 0, cut(p), :] = total + jnp.where(keep, yr[0, cut(p), :], 0.0)
-            send(part.at[i, 0, cut(p)], zr.at[i, cut(p)], BY_Z, zn_recv.at[i], {"blk": at(2 - 4 * i)})
+            send(part.at[i, 0, cut(p)], zr.at[i, cut(p)], BY_Z, zn_recv.at[i, p], {"blk": at(2 - 4 * i)})
 
     def join_y_far(ps):
         for p in ps:
@@ -247,12 +247,13 @@
     for p in (c, d):
         join_z_near(F, 0, [p])
         join_x_own([p])
-    for i in (D, U):
-        pltpu.make_async_remote_copy(
-            src_ref=part.at[i, 0], dst_ref=zr.at[i], send_sem=sends.at[BY_Z], recv_sem=zn_recv.at[i],
-            device_id={"blk": block_of[i]}).wait_recv()
     for p in every:
-        total = part[O, 0, cut(p), :] + zr[D, cut(p), :] + zr[U, cut(p), :]
+        total = part[O, 0, cut(p), :]
+        for i in (U, D):
+            pltpu.make_async_remote_copy(
+                src_ref=part.at[i, 0, cut(p)], dst_ref=zr.at[i, cut(p)], send_sem=sends.at[BY_Z],
+                recv_sem=zn_recv.at[i, p], device_id={"blk": block_of[i]}).wait_recv()
+            total = total + zr[i, cut(p), :]
         for c in x_got[2, p]:
             c.wait_recv()
         for d in far:
@@ -304,7 +305,7 @@
                 dma((far_n, PIECES)),
                 dma((2, PIECES)),
                 dma((far_n, PIECES)),
-                dma((2,)),
+                dma((2, PIECES)),
             ],
             compiler_params=pltpu.CompilerParams(
                 collective_id=0, has_side_effects=True, vmem_limit_bytes=VMEM_BYTES),

time: 29.8 us -> 29.8 us (level)
  no operation moved by 1% of the time
where the time goes in v8:
time: 29.8 us; the launch traced here: 29.7 us
  Pallas kernels  28.9 us (97%)
  local copies, waits for them, and re-layouts  0.71 us (2%)
    pallas_call x1, Pallas kernels, local(): pl.pallas_call(functools.partial(kernel, n_blk, groups), out_shape=jax.Sh...  28.9 us
    unnamed x1, local copies, waits for them, and re-layouts  0.71 us

profile of v8, /device:TPU:0, one launch (start us, length us, event | category | flops | bytes accessed | tf_op | source)
XLA Modules:
  0.0 29.7 jit_solution(11734567479663308640)
XLA Ops:
  0.0 28.9 %shard_map.37 = f32[512,128]{1,0:T(8,128)S(1)} custom-call(s32[16,128]{1,0:T(8,128)} %bitcast.2, s32[16,128]{1,0:T(8,128)} %bitcast.3, f32[2048,128]{1,0:T(8,128)} %pay_ref.1), custom_call_target="tpu_custom_call" | custom-call | tf_op jit(solution)/shard_map/pallas_call | solution.py:283
  28.9 0.7 %copy.5 = f32[512,128]{1,0:T(8,128)} copy(f32[512,128]{1,0:T(8,128)S(1)} %shard_map.37) | data formatting | bytes 524288
